TPU v7x, 32 devices: a whole 2x2x4 slice. The times are simulated.
32 devices in a mesh: section: 2 (over core), expert: 4 (over y, x), tensor: 4 (over z).
Axes of the slice: x: 2, y: 2, z: 4, core: 2. Of those that a mesh axis runs over, the one named last changes fastest.
Arguments:
- inputs: float32 [1, 788, 768], P(None, 'expert'), may hold values from -6 to 6
- cotangent: float32 [1, 788, 768], P(None, 'expert'), may hold values from -6 to 6
- norm_scale: float32 [2, 2, 768], P('section'), may hold values from 0.5 to 1.5
- norm_shift: float32 [2, 2, 768], P('section'), may hold values from -3 to 3
- proj_weight: bfloat16 [2, 768, 3, 768], P('section', None, None, 'tensor'), may hold values from -0.21875 to 0.21875
- proj_bias: float32 [2, 2, 768], P('section', None, 'tensor'), may hold values from -3 to 3
- attn_weight: bfloat16 [2, 768, 768], P('section', 'tensor'), may hold values from -0.75 to 0.75
- attn_bias: float32 [2, 768], P('section'), may hold values from -3 to 3
- expert_in: bfloat16 [2, 4, 768, 3072], P('section', 'expert', None, 'tensor'), may hold values from -0.21875 to 0.21875
- expert_in_bias: float32 [2, 4, 3072], P('section', 'expert', 'tensor'), may hold values from -3 to 3
- expert_out: bfloat16 [2, 4, 3072, 768], P('section', 'expert', 'tensor'), may hold values from -0.109375 to 0.109375
- expert_out_bias: float32 [2, 4, 768], P('section', 'expert'), may hold values from -3 to 3
- routes: int32 [2, 1, 788, 2], P('section', None, 'expert'), may hold values from 0 to 3, all different within a row; in each aligned block of 197 rows (0 to 196, 197 to 393, ..., all dimensions but the last counted through in order) at most 148 rows name the same one
- gate_weights: float32 [2, 1, 788, 2], P('section', None, 'expert'), may hold values from 0.1 to 1
Outputs:
- section_out: float32 [2, 1, 788, 768], P('section', None, 'expert')
- section_in_grad: float32 [2, 1, 788, 768], P('section', None, 'expert')
- grad_norm_scale: float32 [2, 2, 768], P('section')
- grad_norm_shift: float32 [2, 2, 768], P('section')
- grad_proj_weight: float32 [2, 768, 3, 768], P('section', None, None, 'tensor')
- grad_proj_bias: float32 [2, 2, 768], P('section', None, 'tensor')
- grad_attn_weight: float32 [2, 768, 768], P('section', 'tensor')
- grad_attn_bias: float32 [2, 768], P('section')
- grad_expert_in: float32 [2, 4, 768, 3072], P('section', 'expert', None, 'tensor')
- grad_expert_in_bias: float32 [2, 4, 3072], P('section', 'expert', 'tensor')
- grad_expert_out: float32 [2, 4, 3072, 768], P('section', 'expert', 'tensor')
- grad_expert_out_bias: float32 [2, 4, 768], P('section', 'expert')
Inputs may be any that keep to these rules, and one draw needn't show every extreme that they name: `routes`: each row names 2 different experts. In the rows of one index of the expert axis for one section and micro-batch, no expert is named more than 148 times, and in every draw some expert is named exactly 148 times there.
All inputs are finite; a program needn't handle non-finite values.
Results may differ from a plain program's by a relative error of at most 0.015.
Values may be sent and summed in bfloat16 or wider, within the bound.
A program may use at most 128 MiB of HBM per device.

v0:
```python
import jax
import jax.numpy as jnp
from jax import lax
from jax.sharding import PartitionSpec as P

HEAD_DIM = 64
SEQ = 197
TOPK = 2
NORM_EPSILON = 1e-06
GELU_FACTOR = 0.7978845608028654
CUBIC_TERM = 0.044715


def from_behind(block, axis, distance):
    devices = range(lax.axis_size(axis))
    route = [(i - distance, i) for i in devices if i - distance in devices]
    return lax.ppermute(block, axis, route)


def gelu_value(pre_act):
    inner_arg = GELU_FACTOR * (pre_act + CUBIC_TERM * pre_act * pre_act * pre_act)
    return 0.5 * pre_act * (1.0 + jnp.tanh(inner_arg))


def gelu_slope(pre_act):
    tangent = jnp.tanh(GELU_FACTOR * (pre_act + CUBIC_TERM * pre_act * pre_act * pre_act))
    return 0.5 * (1.0 + tangent) + 0.5 * pre_act * (1.0 - tangent * tangent) * GELU_FACTOR * (
        1.0 + 3.0 * CUBIC_TERM * pre_act * pre_act
    )


def layer_norm(values, scale_row, shift_row):
    average = jnp.mean(values, axis=-1, keepdims=True)
    centred = values - average
    variance = jnp.mean(centred * centred, axis=-1, keepdims=True)
    inv_std = lax.rsqrt(variance + NORM_EPSILON)
    normed = centred * inv_std
    return (normed * scale_row + shift_row, normed, inv_std)


def norm_back(grad_normed, normed, inv_std, scale_row):
    scaled = grad_normed * scale_row
    return (
        scaled
        - jnp.mean(scaled, axis=-1, keepdims=True)
        - normed * jnp.mean(scaled * normed, axis=-1, keepdims=True)
    ) * inv_std


def slot_table(route_rows, experts, capacity):
    flat_ids = route_rows.reshape(-1)
    onehot = (flat_ids[:, None] == jnp.arange(experts, dtype=jnp.int32)[None, :]).astype(jnp.int32)
    before = jnp.cumsum(onehot, axis=0) - onehot
    position = jnp.sum(before * onehot, axis=1)
    return flat_ids * capacity + position


def slot_count(row_count, experts):
    return max(2, (3 * TOPK * row_count + 2 * experts - 1) // (2 * experts))


def attend(query_rows, key_rows, value_rows):
    scores = jnp.einsum(
        "ishe,ithe->ihst", query_rows, key_rows, preferred_element_type=jnp.float32
    ) * HEAD_DIM ** (-0.5)
    log_total = jnp.log(jnp.sum(jnp.exp(scores), axis=-1))
    prob_rows = jnp.exp(scores - log_total[..., None]).astype(jnp.bfloat16)
    attn_mixed = jnp.einsum(
        "ihst,ithe->ishe", prob_rows, value_rows, preferred_element_type=jnp.float32
    ).astype(jnp.bfloat16)
    return (attn_mixed, log_total)


def attend_back(query_rows, key_rows, value_rows, attn_mixed, log_total, grad_mixed):
    scale_factor = HEAD_DIM ** (-0.5)
    scores = (
        jnp.einsum("ishe,ithe->ihst", query_rows, key_rows, preferred_element_type=jnp.float32)
        * scale_factor
    )
    prob_f = jnp.exp(scores - log_total[..., None])
    prob_rows = prob_f.astype(jnp.bfloat16)
    grad_values = jnp.einsum(
        "ihst,ishe->ithe", prob_rows, grad_mixed, preferred_element_type=jnp.float32
    )
    grad_probs = jnp.einsum(
        "ishe,ithe->ihst", grad_mixed, value_rows, preferred_element_type=jnp.float32
    )
    row_delta = jnp.einsum(
        "ishe,ishe->ihs", grad_mixed, attn_mixed, preferred_element_type=jnp.float32
    )
    grad_scores = (prob_f * (grad_probs - row_delta[..., None]) * scale_factor).astype(jnp.bfloat16)
    grad_query = jnp.einsum(
        "ihst,ithe->ishe", grad_scores, key_rows, preferred_element_type=jnp.float32
    )
    grad_keys = jnp.einsum(
        "ihst,ishe->ithe", grad_scores, query_rows, preferred_element_type=jnp.float32
    )
    return (grad_query, grad_keys, grad_values)


def hand_over(values, by_step):
    return from_behind(values, "section", by_step)


def forward_block(inputs, weights, route_rows, gate_rows):
    (
        norm_scale,
        norm_shift,
        proj_weight,
        proj_bias,
        attn_weight,
        attn_bias,
        expert_in,
        expert_in_bias,
        expert_out,
        expert_out_bias,
    ) = weights
    row_count, model_width = inputs.shape
    images = row_count // SEQ
    local_width = proj_weight.shape[2]
    head_shape = (images, SEQ, local_width // HEAD_DIM, HEAD_DIM)
    normed_out, normed_first, inv_first = layer_norm(inputs, norm_scale[0], norm_shift[0])
    projected = jnp.einsum(
        "rd,dkf->rkf",
        normed_out.astype(jnp.bfloat16),
        proj_weight,
        preferred_element_type=jnp.float32,
    )
    query_rows = (projected[:, 0] + proj_bias[0]).astype(jnp.bfloat16).reshape(head_shape)
    key_rows = projected[:, 1].astype(jnp.bfloat16).reshape(head_shape)
    value_rows = (projected[:, 2] + proj_bias[1]).astype(jnp.bfloat16).reshape(head_shape)
    attn_mixed, log_total = attend(query_rows, key_rows, value_rows)
    partial_value = jnp.dot(
        attn_mixed.reshape(row_count, local_width), attn_weight, preferred_element_type=jnp.float32
    )
    hidden_res = inputs + (lax.psum(partial_value, "tensor") + attn_bias)
    normed_out_b, normed_second, inv_second = layer_norm(hidden_res, norm_scale[1], norm_shift[1])
    experts = lax.axis_size("expert")
    capacity = slot_count(row_count, experts)
    slot_ids = slot_table(route_rows, experts, capacity)
    repeated = jnp.repeat(normed_out_b.astype(jnp.bfloat16), TOPK, axis=0)
    outgoing = (
        jnp.zeros((experts * capacity, model_width), jnp.bfloat16)
        .at[slot_ids]
        .set(repeated)
        .reshape(experts, capacity, model_width)
    )
    quarter = model_width // lax.axis_size("tensor")
    col_start = lax.axis_index("tensor") * quarter
    bias_part = lax.dynamic_slice_in_dim(expert_out_bias, col_start, quarter, 0)
    incoming = lax.all_to_all(outgoing, "expert", split_axis=0, concat_axis=0, tiled=True)
    pre_act = (
        jnp.einsum("snd,dh->snh", incoming, expert_in, preferred_element_type=jnp.float32)
        + expert_in_bias
    )
    activated = gelu_value(pre_act).astype(jnp.bfloat16)
    partial_out = jnp.einsum(
        "snh,hd->snd", activated, expert_out, preferred_element_type=jnp.float32
    )
    summed = lax.psum_scatter(partial_out, "tensor", scatter_dimension=2, tiled=True)
    produced, pre_act, received = ((summed + bias_part).astype(jnp.bfloat16), pre_act, incoming)
    gate_column = gate_rows.reshape(-1, 1)
    full_rows = lax.all_gather(produced, "tensor", axis=2, tiled=True)
    returned = lax.all_to_all(full_rows, "expert", split_axis=0, concat_axis=0, tiled=True)
    picked = returned.reshape(experts * capacity, model_width)[slot_ids]
    branch = jnp.sum((gate_column * picked).reshape(row_count, TOPK, model_width), axis=1)
    block_out = hidden_res + branch
    kept_state = (
        normed_first,
        inv_first,
        query_rows,
        key_rows,
        value_rows,
        attn_mixed,
        log_total,
        normed_second,
        inv_second,
        slot_ids,
        gate_rows,
        received,
        pre_act,
    )
    return (block_out, kept_state)


def backward_block(cotangent, weights, kept_state):
    (
        norm_scale,
        norm_shift,
        proj_weight,
        proj_bias,
        attn_weight,
        attn_bias,
        expert_in,
        expert_in_bias,
        expert_out,
        expert_out_bias,
    ) = weights
    (
        normed_first,
        inv_first,
        query_rows,
        key_rows,
        value_rows,
        attn_mixed,
        log_total,
        normed_second,
        inv_second,
        slot_ids,
        gate_rows,
        received,
        pre_act,
    ) = kept_state
    row_count, model_width = cotangent.shape
    experts = lax.axis_size("expert")
    capacity = pre_act.shape[1]
    local_width = proj_weight.shape[2]
    quarter = model_width // lax.axis_size("tensor")
    grad_rows = (
        (gate_rows.reshape(row_count, TOPK, 1) * cotangent[:, None, :])
        .astype(jnp.bfloat16)
        .reshape(TOPK * row_count, model_width)
    )
    outgoing = (
        jnp.zeros((experts * capacity, model_width), jnp.bfloat16)
        .at[slot_ids]
        .set(grad_rows)
        .reshape(experts, capacity, model_width)
    )
    grad_out = lax.all_to_all(outgoing, "expert", split_axis=0, concat_axis=0, tiled=True)
    activated = gelu_value(pre_act).astype(jnp.bfloat16)
    grad_expert_out = jnp.einsum(
        "snh,snd->hd", activated, grad_out, preferred_element_type=jnp.float32
    )
    grad_expert_out_bias = jnp.sum(grad_out, axis=(0, 1), dtype=jnp.float32)
    grad_pre = jnp.einsum(
        "snd,hd->snh", grad_out, expert_out, preferred_element_type=jnp.float32
    ) * gelu_slope(pre_act)
    grad_expert_in_bias = jnp.sum(grad_pre, axis=(0, 1))
    grad_pre_b = grad_pre.astype(jnp.bfloat16)
    grad_expert_in = jnp.einsum(
        "snd,snh->dh", received, grad_pre_b, preferred_element_type=jnp.float32
    )
    partial_in = jnp.einsum(
        "snh,dh->snd", grad_pre_b, expert_in, preferred_element_type=jnp.float32
    )
    grad_buffer = lax.psum_scatter(partial_in, "tensor", scatter_dimension=2, tiled=True).astype(
        jnp.bfloat16
    )
    returned = lax.all_to_all(grad_buffer, "expert", split_axis=0, concat_axis=0, tiled=True)
    picked = returned.reshape(experts * capacity, quarter)[slot_ids]
    grad_cols = jnp.sum(picked.reshape(row_count, TOPK, quarter), axis=1, dtype=jnp.float32)
    grad_normed_b = lax.all_gather(grad_cols, "tensor", axis=1, tiled=True)
    grad_hidden = cotangent + norm_back(grad_normed_b, normed_second, inv_second, norm_scale[1])
    grad_hidden_b = grad_hidden.astype(jnp.bfloat16)
    grad_attn_bias = jnp.sum(grad_hidden, axis=0)
    mixed_flat = attn_mixed.reshape(row_count, local_width)
    grad_attn_weight = jnp.einsum(
        "rf,rd->fd", mixed_flat, grad_hidden_b, preferred_element_type=jnp.float32
    )
    grad_mixed = (
        jnp.einsum("rd,fd->rf", grad_hidden_b, attn_weight, preferred_element_type=jnp.float32)
        .astype(jnp.bfloat16)
        .reshape(attn_mixed.shape)
    )
    grad_query, grad_keys, grad_values = attend_back(
        query_rows, key_rows, value_rows, attn_mixed, log_total, grad_mixed
    )
    query_flat = grad_query.reshape(row_count, local_width)
    key_flat = grad_keys.reshape(row_count, local_width)
    value_flat = grad_values.reshape(row_count, local_width)
    grad_proj_bias = jnp.stack([jnp.sum(query_flat, axis=0), jnp.sum(value_flat, axis=0)])
    grad_proj = jnp.stack([query_flat, key_flat, value_flat], axis=1).astype(jnp.bfloat16)
    normed_a = (normed_first * norm_scale[0] + norm_shift[0]).astype(jnp.bfloat16)
    grad_proj_weight = jnp.einsum(
        "rd,rkf->dkf", normed_a, grad_proj, preferred_element_type=jnp.float32
    )
    partial_norm = jnp.einsum(
        "rkf,dkf->rd", grad_proj, proj_weight, preferred_element_type=jnp.float32
    )
    grad_normed_a = lax.psum(partial_norm, "tensor")
    grad_input = grad_hidden + norm_back(grad_normed_a, normed_first, inv_first, norm_scale[0])
    grad_norm_scale = jnp.stack(
        [
            jnp.sum(grad_normed_a * normed_first, axis=0),
            jnp.sum(grad_normed_b * normed_second, axis=0),
        ]
    )
    grad_norm_shift = jnp.stack([jnp.sum(grad_normed_a, axis=0), jnp.sum(grad_normed_b, axis=0)])
    mixer_part = (
        grad_norm_scale,
        grad_norm_shift,
        grad_proj_weight,
        grad_proj_bias,
        grad_attn_weight,
        grad_attn_bias,
    )
    expert_part = (grad_expert_in, grad_expert_in_bias, grad_expert_out, grad_expert_out_bias)
    return (grad_input, mixer_part, expert_part)


def on_device(
    inputs,
    cotangent,
    norm_scale,
    norm_shift,
    proj_weight,
    proj_bias,
    attn_weight,
    attn_bias,
    expert_in,
    expert_in_bias,
    expert_out,
    expert_out_bias,
    routes,
    gate_weights,
):
    weights = (
        norm_scale[0],
        norm_shift[0],
        proj_weight[0],
        proj_bias[0],
        attn_weight[0],
        attn_bias[0],
        expert_in[0, 0],
        expert_in_bias[0, 0],
        expert_out[0, 0],
        expert_out_bias[0, 0],
    )
    section_id = lax.axis_index("section")
    is_first = section_id == 0
    micro_count = inputs.shape[0]
    received = jnp.zeros_like(inputs[0])
    saved_keeps = []
    produced = []
    for tick_index in range(micro_count + 1):
        own_micro = jnp.clip(tick_index - section_id, 0, micro_count - 1)
        block_in = jnp.where(is_first, inputs[min(tick_index, micro_count - 1)], received)
        route_rows = lax.dynamic_index_in_dim(routes[0], own_micro, 0, keepdims=False)
        gate_rows = lax.dynamic_index_in_dim(gate_weights[0], own_micro, 0, keepdims=False)
        block_out, kept_state = forward_block(block_in, weights, route_rows, gate_rows)
        saved_keeps.append(kept_state)
        produced.append(block_out)
        if tick_index < micro_count:
            received = hand_over(block_out, 1)
    sent_back = jnp.zeros_like(inputs[0])
    mixer_sums = None
    expert_sums = None
    input_grads = []
    for tick_index in range(micro_count + 1):
        last_cotangent = cotangent[min(tick_index, micro_count - 1)]
        if tick_index == micro_count:
            last_cotangent = jnp.zeros_like(last_cotangent)
        block_grad = jnp.where(is_first, sent_back, last_cotangent)
        kept_state = jax.tree.map(
            lambda later_keep, early_keep: jnp.where(is_first, early_keep, later_keep),
            saved_keeps[min(tick_index + 1, micro_count)],
            saved_keeps[max(tick_index - 1, 0)],
        )
        grad_input, mixer_part, expert_part = backward_block(block_grad, weights, kept_state)
        mixer_sums = (
            mixer_part if mixer_sums is None else jax.tree.map(jnp.add, mixer_sums, mixer_part)
        )
        expert_sums = (
            expert_part if expert_sums is None else jax.tree.map(jnp.add, expert_sums, expert_part)
        )
        input_grads.append(grad_input)
        if tick_index < micro_count:
            sent_back = hand_over(grad_input, -1)
    section_out = jnp.stack([jnp.where(is_first, produced[0], produced[1])])
    section_in_grad = jnp.stack([jnp.where(is_first, input_grads[1], input_grads[0])])
    scale_sum, shift_sum, proj_sum, proj_bias_sum, attn_sum_w, attn_bias_sum = mixer_sums
    totals = lax.psum(
        (scale_sum, shift_sum, proj_sum, proj_bias_sum, attn_sum_w, attn_bias_sum), "expert"
    )
    grad_in_w, grad_in_b, grad_out_w, grad_out_b = expert_sums
    return (
        section_out[None],
        section_in_grad[None],
        totals[0][None],
        totals[1][None],
        totals[2][None],
        totals[3][None],
        totals[4][None],
        totals[5][None],
        grad_in_w[None, None],
        grad_in_b[None, None],
        grad_out_w[None, None],
        grad_out_b[None, None],
    )


def solution(mesh):
    in_specs = (
        P(None, "expert", None),
        P(None, "expert", None),
        P("section", None, None),
        P("section", None, None),
        P("section", None, None, "tensor"),
        P("section", None, "tensor"),
        P("section", "tensor", None),
        P("section", None),
        P("section", "expert", None, "tensor"),
        P("section", "expert", "tensor"),
        P("section", "expert", "tensor", None),
        P("section", "expert", None),
        P("section", None, "expert", None),
        P("section", None, "expert", None),
    )
    out_specs = (
        P("section", None, "expert", None),
        P("section", None, "expert", None),
        P("section", None, None),
        P("section", None, None),
        P("section", None, None, "tensor"),
        P("section", None, "tensor"),
        P("section", "tensor", None),
        P("section", None),
        P("section", "expert", None, "tensor"),
        P("section", "expert", "tensor"),
        P("section", "expert", "tensor", None),
        P("section", "expert", None),
    )
    return jax.shard_map(
        on_device, mesh=mesh, in_specs=in_specs, out_specs=out_specs, check_vma=False
    )
```

profile of v0, /device:TPU:0, one launch (start us, length us, event | category | flops | bytes accessed | tf_op | source)
XLA Modules:
  0.0 782.8 jit_solution(3827961485082313167)
XLA Ops:
  18.0 40.3 %all-reduce.9.cloned.1.call-done = f32[197,768]{1,0:T(8,128)} async-done(((f32[197,768]{1,0:T(8,128)}), f32[197,768]{1,0:T(8,128)}) %all-reduce.9.cloned.1.call-update) | async-done | bytes 605200 | tf_op jit(solution)/shard_map/psum | solution.py:136
  62.0 3.0 scatter_custom_fusion
  66.1 4.2 all-to-all-start
  70.5 12.0 %all-to-all-done = bf16[4,148,768]{2,1,0:T(8,128)(2,1)} async-done(((bf16[4,148,768]{2,1,0:T(8,128)(2,1)}), bf16[4,148,768]{2,1,0:T(8,128)(2,1)}, u32[]{:S(2)}, u32[]{:S(2)}) %all-to-all-start) | async-done | bytes 909344 | tf_op jit(solution)/shard_map/all_to_all | solution.py:151
  86.0 2.6 fusion.30
  88.5 4.3 copy.142
  92.8 4.5 reshape.717
  98.1 39.8 %reduce-scatter.13.cloned.1.call-done = f32[192,592]{1,0:T(8,128)} async-done(((f32[768,592]{1,0:T(8,128)}), f32[192,592]{1,0:T(8,128)}) %reduce-scatter.13.cloned.1.call-update) | async-done | bytes 454672
  142.2 29.4 %all_gather.12 = bf16[4,148,768]{1,0,2:T(4,128)(2,1)} all-gather(bf16[4,148,192]{1,0,2:T(4,128)(2,1)S(1)} %copy.93), channel_id=1, replica_groups=mesh['section'=2,'expert'=4,'tensor'=4] {'tensor'}, dimensions={2}, use_global_device_ids=true | all-gather | bytes 1136640 | tf_op jit(solution)/shard_map/all_gather | solution.py:163
  171.5 3.5 copy.94
  175.0 4.2 all-to-all-start.1
  180.3 9.9 %all-to-all-done.1 = bf16[4,148,768]{2,1,0:T(8,128)(2,1)} async-done(((bf16[4,148,768]{2,1,0:T(8,128)(2,1)}), bf16[4,148,768]{2,1,0:T(8,128)(2,1)}, u32[]{:S(2)}, u32[]{:S(2)}) %all-to-all-start.1) | async-done | bytes 909344 | tf_op jit(solution)/shard_map/all_to_all | solution.py:164
  191.6 2.7 gather_fusion
  194.3 2.8 reshape.627
  197.1 2.8 multiply_reduce_fusion.1
  207.2 40.7 %all-reduce.11.cloned.1.call-done = f32[197,768]{1,0:T(8,128)} async-done(((f32[197,768]{1,0:T(8,128)}), f32[197,768]{1,0:T(8,128)}) %all-reduce.11.cloned.1.call-update) | async-done | bytes 605200 | tf_op jit(solution)/shard_map/psum | solution.py:136
  252.2 3.0 scatter_custom_fusion.1
  256.4 4.8 all-to-all-start.2
  262.8 3.0 mul.457
  265.9 3.3 scatter_custom_fusion.2
  270.3 3.0 all-to-all-done.2
  273.2 3.5 all-to-all-start.4
  276.8 4.6 multiply_convert_fusion
  281.4 7.3 all-to-all-done.4
  288.7 5.2 fusion.129
  297.0 4.3 copy.146
  301.3 4.5 reshape.721
  306.5 4.4 fusion.28
  310.9 4.3 copy.144
  315.2 4.5 reshape.719
  319.8 26.7 %reduce-scatter.17.cloned.1.call-done = f32[192,592]{1,0:T(8,128)} async-done(((f32[768,592]{1,0:T(8,128)}), f32[192,592]{1,0:T(8,128)}) %reduce-scatter.17.cloned.1.call-update) | async-done | bytes 454672
  348.8 4.1 all-to-all-start.5
  352.9 37.0 %reduce-scatter.15.cloned.1.call-done = f32[192,592]{1,0:T(8,128)} async-done(((f32[768,592]{1,0:T(8,128)}), f32[192,592]{1,0:T(8,128)}) %reduce-scatter.15.cloned.1.call-update) | async-done | bytes 454672
  394.1 29.4 %all_gather.13 = bf16[4,148,768]{1,0,2:T(4,128)(2,1)} all-gather(bf16[4,148,192]{1,0,2:T(4,128)(2,1)S(1)} %copy.96), channel_id=1, replica_groups=mesh['section'=2,'expert'=4,'tensor'=4] {'tensor'}, dimensions={2}, use_global_device_ids=true | all-gather | bytes 1136640 | tf_op jit(solution)/shard_map/all_gather | solution.py:163
  423.5 3.5 copy.97
  427.0 4.3 all-to-all-start.3
  437.4 19.4 %all_gather.14 = f32[197,768]{0,1:T(8,128)S(1)} all-gather(f32[197,192]{0,1:T(8,128)S(1)} %copy.100), channel_id=1, replica_groups=mesh['section'=2,'expert'=4,'tensor'=4] {'tensor'}, dimensions={1}, use_global_device_ids=true | all-gather | bytes 756480 | tf_op jit(solution)/shard_map/all_gather | solution.py:253
  459.3 2.7 gather_fusion.1
  462.0 2.8 reshape.628
  464.8 2.9 multiply_reduce_fusion
  475.6 39.6 %all-reduce.13.cloned.1.call-done = f32[197,768]{1,0:T(8,128)} async-done(((f32[197,768]{1,0:T(8,128)}), f32[197,768]{1,0:T(8,128)}) %all-reduce.13.cloned.1.call-update) | async-done | bytes 605200 | tf_op jit(solution)/shard_map/psum | solution.py:281
  519.7 2.6 collective-permute-done.1
  524.6 3.0 mul.490
  527.6 4.0 scatter_custom_fusion.3
  531.6 2.3 reshape.622
  533.9 17.6 %all_to_all.40 = bf16[4,148,768]{2,1,0:T(8,128)(2,1)S(1)} all-to-all(bf16[4,148,768]{2,1,0:T(8,128)(2,1)} %reshape.622), channel_id=1, replica_groups=mesh['section'=2,'expert'=4,'tensor'=4] {'expert'}, dimensions={0} | all-to-all | bytes 1818624 | tf_op jit(solution)/shard_map/all_to_all | solution.py:230
  551.5 4.9 fusion.130
  559.6 4.3 copy.148
  563.8 4.5 reshape.723
  569.8 4.2 fusion.61
  575.8 32.2 %reduce-scatter.19.cloned.1.call-done = f32[192,592]{1,0:T(8,128)} async-done(((f32[768,592]{1,0:T(8,128)}), f32[192,592]{1,0:T(8,128)}) %reduce-scatter.19.cloned.1.call-update) | async-done | bytes 454672
  610.4 3.7 all-to-all-start.7
  614.0 2.6 fusion.103
  616.6 2.9 all-to-all-done.7
  619.6 2.6 gather_fusion.3
  628.1 18.3 %all_gather.15 = f32[197,768]{0,1:T(8,128)} all-gather(f32[197,192]{0,1:T(8,128)} %copy.107), channel_id=1, replica_groups=mesh['section'=2,'expert'=4,'tensor'=4] {'tensor'}, dimensions={1}, use_global_device_ids=true | all-gather | bytes 756480 | tf_op jit(solution)/shard_map/all_gather | solution.py:253
  658.9 4.1 fusion.131
  663.4 2.6 copy.115
  667.4 4.4 fusion
  671.8 3.9 fusion.1
  676.0 18.1 %all-reduce.15.cloned.1.call-done = f32[197,768]{1,0:T(8,128)} async-done(((f32[197,768]{1,0:T(8,128)}), f32[197,768]{1,0:T(8,128)}) %all-reduce.15.cloned.1.call-update) | async-done | bytes 605200 | tf_op jit(solution)/shard_map/psum | solution.py:281
  698.4 17.9 %all-reduce.1 = (f32[1,2,768]{2,1,0:T(2,128)}, f32[1,2,768]{2,1,0:T(2,128)}, f32[1,2,192]{2,1,0:T(2,128)}, f32[1,768]{1,0:T(1,128)}) all-reduce(f32[1,2,768]{2,1,0:T(2,128)S(1)} %fusion.106, f32[1,2,768]{2,1,0:T(2,128)S(1)} %fusion.107, f32[1,2,192]{2,1,0:T(2,128)S(1)} %fusion.108, ...), channel_id=1, replica_groups=mesh['section'=2,'expert'=4,'tensor'=4] {'expert'}, use_global_device_ids=true, to_apply=%region_41.42 | all-reduce | flops 4224 | bytes 33792 | tf_op jit(solution)/shard_map/psum | solution.py:373
  716.3 55.8 %all-reduce.17.cloned.1.call-done = (f32[1,768,3,192]{1,3,2,0:T(8,128)}, f32[1,192,768]{2,1,0:T(8,128)}) async-done(((f32[1,768,3,192]{1,3,2,0:T(8,128)}, f32[1,192,768]{2,1,0:T(8,128)}), (f32[1,768,3,192]{1,3,2,0:T(8,128)}, f32[1,192,768]{2,1,0:T(8,128)})) %all-reduce.17.cloned.1.call-update) | async-done | bytes 2359312 | tf_op jit(solution)/shard_map/psum | solution.py:373
  772.1 2.9 copy.183
  (418 shorter events, 108.5 us)
Async XLA Ops:
  7.2 75.3 %copy-start = (bf16[1,1,768,768]{3,2,1,0:T(8,128)(2,1)S(1)}, bf16[1,1,768,768]{3,2,1,0:T(8,128)(2,1)}, u32[]{:S(2)}) copy-start(bf16[1,1,768,768]{3,2,1,0:T(8,128)(2,1)} %param.22) | copy-start | bytes 3538948
  7.2 51.1 %all-reduce.9.cloned.1.call-start = ((), (), s32[]{:S(2)}) async-start(), calls=%async_computation.12 | async-start | bytes 1228800 | tf_op jit(solution)/shard_map/psum | solution.py:136
  8.5 4.9 copy-start.78
  8.5 4.9 copy-start.106
  13.6 191.1 %copy-start.65 = (f32[3,64]{1,0:T(4,128)}, f32[3,64]{1,0:T(4,128)S(1)}, u32[]{:S(2)}) copy-start(f32[3,64]{1,0:T(4,128)S(1)} %add.382) | copy-start | bytes 2308
  14.0 44.3 %copy-start.2 = (f32[1,197,768]{2,0,1:T(1,128)S(1)}, f32[1,197,768]{2,0,1:T(1,128)}, u32[]{:S(2)}) copy-start(f32[1,197,768]{2,0,1:T(1,128)} %param.14) | copy-start | bytes 1815556
  14.2 45.3 %copy-start.32 = (bf16[197,3,64]{0,2,1:T(8,128)(2,1)}, bf16[197,3,64]{0,2,1:T(8,128)(2,1)S(1)}, u32[]{:S(2)}) copy-start(bf16[197,3,64]{0,2,1:T(8,128)(2,1)S(1)} %add_convert_fusion.11) | copy-start | bytes 226948
  14.4 45.1 %copy-start.54 = (bf16[3,64,197]{2,1,0:T(8,128)(2,1)}, bf16[3,64,197]{2,1,0:T(8,128)(2,1)S(1)}, u32[]{:S(2)}) copy-start(bf16[3,64,197]{2,1,0:T(8,128)(2,1)S(1)} %convolution_convert_fusion.5) | copy-start | bytes 226948
  18.0 44.1 %copy-start.95 = (s32[394,1]{0,1:T(1,128)}, s32[394,1]{0,1:T(1,128)S(1)}, u32[]{:S(2)}) copy-start(s32[394,1]{0,1:T(1,128)S(1)} %compare_select_fusion) | copy-start | bytes 4732
  59.5 5.5 copy-start.71
  59.8 5.3 copy-start.87
  59.8 5.2 copy-start.79
  65.0 5.4 copy-start.105
  66.1 16.4 %all-to-all-start = ((bf16[4,148,768]{2,1,0:T(8,128)(2,1)}), bf16[4,148,768]{2,1,0:T(8,128)(2,1)}, u32[]{:S(2)}, u32[]{:S(2)}) async-start(bf16[4,148,768]{2,1,0:T(8,128)(2,1)} %reshape.612), calls=%async_computation | async-start | bytes 1867776 | tf_op jit(solution)/shard_map/all_to_all | solution.py:151
  70.4 67.6 %reduce-scatter.13.cloned.1.call-start = ((), (), s32[]{:S(2)}) async-start(), calls=%async_computation.16 | async-start | bytes 2457600
  70.5 14.2 %copy-start.101 = (f32[768]{0:T(1024)}, f32[768]{0:T(1024)S(1)}, u32[]{:S(2)}) copy-start(f32[768]{0:T(1024)S(1)} %reduce.18) | copy-start | bytes 9220
  98.1 44.0 %copy-start.89 = (f32[1,1,192]{2,1,0:T(1,128)}, f32[1,1,192]{2,1,0:T(1,128)S(1)}, u32[]{:S(2)}) copy-start(f32[1,1,192]{2,1,0:T(1,128)S(1)} %constant_dynamic-slice_fusion) | copy-start | bytes 2308
  171.5 8.0 %copy-start.93 = (f32[1,1,197,2]{2,3,1,0:T(2,128)S(1)}, f32[1,1,197,2]{2,3,1,0:T(2,128)}, u32[]{:S(2)}) copy-start(f32[1,1,197,2]{2,3,1,0:T(2,128)} %param.27) | copy-start | bytes 4732
  171.5 8.8 %copy-start.96 = (s32[394,1]{0,1:T(1,128)S(1)}, s32[394,1]{0,1:T(1,128)}, u32[]{:S(2)}) copy-start(s32[394,1]{0,1:T(1,128)} %copy-done.95) | copy-start | bytes 4732
  175.0 15.2 %all-to-all-start.1 = ((bf16[4,148,768]{2,1,0:T(8,128)(2,1)}), bf16[4,148,768]{2,1,0:T(8,128)(2,1)}, u32[]{:S(2)}, u32[]{:S(2)}) async-start(bf16[4,148,768]{2,1,0:T(8,128)(2,1)} %copy.94), calls=%async_computation.1 | async-start | bytes 1867776 | tf_op jit(solution)/shard_map/all_to_all | solution.py:164
  179.3 68.6 %all-reduce.11.cloned.1.call-start = ((), (), s32[]{:S(2)}) async-start(), calls=%async_computation.13 | async-start | bytes 1228800 | tf_op jit(solution)/shard_map/psum | solution.py:136
  200.0 3.1 collective-permute-start
  205.8 43.3 %copy-start.34 = (bf16[197,3,64]{0,2,1:T(8,128)(2,1)}, bf16[197,3,64]{0,2,1:T(8,128)(2,1)S(1)}, u32[]{:S(2)}) copy-start(bf16[197,3,64]{0,2,1:T(8,128)(2,1)S(1)} %add_convert_fusion.9) | copy-start | bytes 226948
  206.0 43.4 %copy-start.56 = (bf16[3,64,197]{2,1,0:T(8,128)(2,1)}, bf16[3,64,197]{2,1,0:T(8,128)(2,1)S(1)}, u32[]{:S(2)}) copy-start(bf16[3,64,197]{2,1,0:T(8,128)(2,1)S(1)} %convolution_convert_fusion.4) | copy-start | bytes 226948
  206.1 43.3 %copy-start.88 = (f32[197]{0:T(256)S(1)}, f32[197]{0:T(256)}, u32[]{:S(2)}) copy-start(f32[197]{0:T(256)} %copy-done.87) | copy-start | bytes 2368
  249.2 6.1 copy-start.73
  250.0 5.2 copy-start.83
  255.2 5.9 copy-start.94
  256.4 4.9 copy-start.27
  256.4 16.9 %all-to-all-start.2 = ((bf16[4,148,768]{2,1,0:T(8,128)(2,1)}), bf16[4,148,768]{2,1,0:T(8,128)(2,1)}, u32[]{:S(2)}, u32[]{:S(2)}) async-start(bf16[4,148,768]{2,1,0:T(8,128)(2,1)} %reshape.616), calls=%async_computation.2 | async-start | bytes 1867776 | tf_op jit(solution)/shard_map/all_to_all | solution.py:151
  273.2 15.4 %all-to-all-start.4 = ((bf16[4,148,768]{2,1,0:T(8,128)(2,1)}), bf16[4,148,768]{2,1,0:T(8,128)(2,1)S(1)}, u32[]{:S(2)}, u32[]{:S(2)}) async-start(bf16[4,148,768]{2,1,0:T(8,128)(2,1)} %reshape.618), calls=%async_computation.4 | async-start | bytes 1867776 | tf_op jit(solution)/shard_map/all_to_all | solution.py:230
  276.8 69.7 %reduce-scatter.17.cloned.1.call-start = ((), (), s32[]{:S(2)}) async-start(), calls=%async_computation.18 | async-start | bytes 2457600
  288.7 5.2 copy-start.19
  305.9 84.1 %reduce-scatter.15.cloned.1.call-start = ((), (), s32[]{:S(2)}) async-start(), calls=%async_computation.17 | async-start | bytes 2457600
  347.8 44.9 %copy-start.90 = (f32[1,1,192]{2,1,0:T(1,128)S(1)}, f32[1,1,192]{2,1,0:T(1,128)}, u32[]{:S(2)}) copy-start(f32[1,1,192]{2,1,0:T(1,128)} %copy-done.89) | copy-start | bytes 2308
  348.8 78.2 %all-to-all-start.5 = ((bf16[4,148,192]{2,1,0:T(8,128)(2,1)}), bf16[4,148,192]{2,1,0:T(8,128)(2,1)}, u32[]{:S(2)}, u32[]{:S(2)}) async-start(bf16[4,148,192]{2,1,0:T(8,128)(2,1)} %copy.147), calls=%async_computation.5 | async-start | bytes 622592 | tf_op jit(solution)/shard_map/all_to_all | solution.py:250
  423.5 8.0 %copy-start.31 = (f32[197,1,192]{0,2,1:T(8,128)S(1)}, f32[197,1,192]{0,2,1:T(8,128)}, u32[]{:S(2)}) copy-start(f32[197,1,192]{0,2,1:T(8,128)} %copy-done.30) | copy-start | bytes 453892
  423.5 8.0 %copy-start.51 = (bf16[197,1,192]{0,2,1:T(8,128)(2,1)S(1)}, bf16[197,1,192]{0,2,1:T(8,128)(2,1)}, u32[]{:S(2)}) copy-start(bf16[197,1,192]{0,2,1:T(8,128)(2,1)} %copy-done.50) | copy-start | bytes 226948
  423.5 8.0 %copy-start.53 = (bf16[197,1,192]{0,2,1:T(8,128)(2,1)S(1)}, bf16[197,1,192]{0,2,1:T(8,128)(2,1)}, u32[]{:S(2)}) copy-start(bf16[197,1,192]{0,2,1:T(8,128)(2,1)} %copy-done.52) | copy-start | bytes 226948
  423.5 8.0 %copy-start.66 = (f32[3,64]{1,0:T(4,128)S(1)}, f32[3,64]{1,0:T(4,128)}, u32[]{:S(2)}) copy-start(f32[3,64]{1,0:T(4,128)} %copy-done.65) | copy-start | bytes 2308
  427.0 5.2 copy-start.75
  427.0 30.9 %all-to-all-start.3 = ((bf16[4,148,768]{2,1,0:T(8,128)(2,1)}), bf16[4,148,768]{2,1,0:T(8,128)(2,1)}, u32[]{:S(2)}, u32[]{:S(2)}) async-start(bf16[4,148,768]{2,1,0:T(8,128)(2,1)} %copy.97), calls=%async_computation.3 | async-start | bytes 1867776 | tf_op jit(solution)/shard_map/all_to_all | solution.py:164
  431.4 83.9 %all-reduce.13.cloned.1.call-start = ((), (), s32[]{:S(2)}) async-start(), calls=%async_computation.14 | async-start | bytes 1228800 | tf_op jit(solution)/shard_map/psum | solution.py:281
  461.9 5.8 copy-start.4
  461.9 5.8 copy-start.72
  461.9 5.8 copy-start.74
  461.9 5.8 copy-start.80
  462.0 5.8 copy-start.84
  472.7 42.6 %copy-start.70 = (f32[197]{0:T(256)S(1)}, f32[197]{0:T(256)}, u32[]{:S(2)}) copy-start(f32[197]{0:T(256)} %copy-done.69) | copy-start | bytes 2368
  472.7 42.6 %copy-start.77 = (f32[197]{0:T(256)S(1)}, f32[197]{0:T(256)}, u32[]{:S(2)}) copy-start(f32[197]{0:T(256)} %copy-done.76) | copy-start | bytes 2368
  475.6 132.5 %reduce-scatter.19.cloned.1.call-start = ((), (), s32[]{:S(2)}) async-start(), calls=%async_computation.19 | async-start | bytes 2457600
  518.4 9.2 %copy-start.25 = (f32[197,768]{1,0:T(8,128)}, f32[197,768]{1,0:T(8,128)S(1)}, u32[]{:S(2)}) copy-start(f32[197,768]{1,0:T(8,128)S(1)} %multiply_add_fusion.4) | copy-start | bytes 1815556
  518.4 3.9 collective-permute-start.1
  531.6 19.9 %copy-start.103 = (f32[768]{0:T(1024)S(1)}, f32[768]{0:T(1024)}, u32[]{:S(2)}) copy-start(f32[768]{0:T(1024)} %copy-done.101) | copy-start | bytes 9220
  533.9 17.7 %copy-start.108 = (bf16[1,1,768,768]{3,2,1,0:T(8,128)(2,1)S(1)}, bf16[1,1,768,768]{3,2,1,0:T(8,128)(2,1)}, u32[]{:S(2)}) copy-start(bf16[1,1,768,768]{3,2,1,0:T(8,128)(2,1)} %param.24) | copy-start | bytes 3538948
  551.5 4.9 copy-start.20
  569.8 5.0 copy-start.6
  569.8 5.0 copy-start.42
  610.4 9.2 %all-to-all-start.7 = ((bf16[4,148,192]{2,1,0:T(8,128)(2,1)}), bf16[4,148,192]{2,1,0:T(8,128)(2,1)S(1)}, u32[]{:S(2)}, u32[]{:S(2)}) async-start(bf16[4,148,192]{2,1,0:T(8,128)(2,1)} %copy.149), calls=%async_computation.7 | async-start | bytes 622592 | tf_op jit(solution)/shard_map/all_to_all | solution.py:250
  614.0 80.1 %all-reduce.15.cloned.1.call-start = ((), (), s32[]{:S(2)}) async-start(), calls=%async_computation.15 | async-start | bytes 1228800 | tf_op jit(solution)/shard_map/psum | solution.py:281
  622.2 26.4 %copy-start.8 = (f32[197,768]{1,0:T(8,128)S(1)}, f32[197,768]{1,0:T(8,128)}, u32[]{:S(2)}) copy-start(f32[197,768]{1,0:T(8,128)} %copy-done.7) | copy-start | bytes 1815556
  655.6 116.5 %all-reduce.17.cloned.1.call-start = ((), (), s32[]{:S(2)}) async-start(), calls=%async_computation.20 | async-start | bytes 4718592 | tf_op jit(solution)/shard_map/psum | solution.py:373
  658.9 4.5 copy-start.92
  675.7 19.9 %copy-start.81 = (f32[197]{0:T(256)S(1)}, f32[197]{0:T(256)}, u32[]{:S(2)}) copy-start(f32[197]{0:T(256)} %get-tuple-element.115) | copy-start | bytes 2368
  (69 other events, 160.8 us)
Sparse Core Ops, SparseCore 0:
  15.7 42.5 all-reduce.8
  97.5 40.4 reduce-scatter.12
  207.3 40.5 all-reduce.10
  306.0 40.4 reduce-scatter.16
  349.2 40.6 reduce-scatter.14
  475.7 39.5 all-reduce.12
  568.5 39.4 reduce-scatter.18
  655.7 38.4 all-reduce.14
  697.9 74.1 all-reduce.16
where the time goes:
time: 794 us; the launch traced here: 783 us
  waiting for transfers between devices  370 us (47%)
  blocking collectives  132 us (17%)
  local copies, waits for them, and re-layouts  126 us (16%)
  matrix products  63.3 us (8%)
  other arithmetic  43 us (5%)
  starting transfers between devices  32.6 us (4%)
  between operations  16.1 us (2%)
    unnamed x13, waiting for transfers between devices  136 us
    psum x2, waiting for transfers between devices, forward_block(): hidden_res = inputs + (lax.psum(partial_value, 'tensor') + attn_bias)  81 us
    unnamed x253, local copies, waits for them, and re-layouts  61.4 us
    all_gather x2, blocking collectives, forward_block(): full_rows = lax.all_gather(produced, 'tensor', axis=2, tiled=True)  58.7 us
    psum x2, waiting for transfers between devices, backward_block(): grad_normed_a = lax.psum(partial_norm, 'tensor')  57.8 us
    psum x1, waiting for transfers between devices, on_device(): lax.psum((scale_sum, shift_sum, proj_sum, proj_bias_sum, attn_sum_w, attn...  55.8 us
    all_gather x2, blocking collectives, backward_block(): grad_normed_b = lax.all_gather(grad_cols, 'tensor', axis=1, tiled=True)  37.7 us
    psum x1, blocking collectives, on_device(): lax.psum((scale_sum, shift_sum, proj_sum, proj_bias_sum, attn_sum_w, attn...  17.9 us
  transfers between devices with their start and end apart: 18, of which 16 were waited for; matrix products, arithmetic and copies ran while one was open for 10% of the time, Pallas kernels for 0%

commit v1 on v0

--- a/solution.py
+++ b/solution.py
@@ -9,6 +9,12 @@
 NORM_EPSILON = 1e-06
 GELU_FACTOR = 0.7978845608028654
 CUBIC_TERM = 0.044715
+
+
+def add_all(x, axis):
+    shards = lax.all_gather(x, axis, axis=0, tiled=False)
+    total = shards.sum(axis=0)
+    return total
 
 
 def from_behind(block, axis, distance):
@@ -133,7 +139,7 @@
     partial_value = jnp.dot(
         attn_mixed.reshape(row_count, local_width), attn_weight, preferred_element_type=jnp.float32
     )
-    hidden_res = inputs + (lax.psum(partial_value, "tensor") + attn_bias)
+    hidden_res = inputs + (add_all(partial_value, "tensor") + attn_bias)
     normed_out_b, normed_second, inv_second = layer_norm(hidden_res, norm_scale[1], norm_shift[1])
     experts = lax.axis_size("expert")
     capacity = slot_count(row_count, experts)

time: 794 us -> 820 us (1.033)
  waiting for transfers between devices: 370 us -> 393 us
    all_gather x0 -> x2, waiting for transfers between devices: none -> 105 us  [add_all(): shards = lax.all_gather(x, axis, axis=0, tiled=False)]
    psum x2 -> x0, waiting for transfers between devices: 81 us -> none  [forward_block(): hidden_res = inputs + (lax.psum(partial_value, 'tensor') + attn_bias)]
where the time goes in v1:
time: 820 us; the launch traced here: 808 us
  waiting for transfers between devices  393 us (48%)
  blocking collectives  132 us (16%)
  local copies, waits for them, and re-layouts  126 us (15%)
  matrix products  63.2 us (8%)
  other arithmetic  44.7 us (5%)
  starting transfers between devices  32.6 us (4%)
  between operations  16.1 us (2%)
    unnamed x13, waiting for transfers between devices  134 us
    all_gather x2, waiting for transfers between devices, add_all(): shards = lax.all_gather(x, axis, axis=0, tiled=False)  105 us
    unnamed x253, local copies, waits for them, and re-layouts  61.6 us
    all_gather x2, blocking collectives, forward_block(): full_rows = lax.all_gather(produced, 'tensor', axis=2, tiled=True)  58.7 us
    psum x2, waiting for transfers between devices, backward_block(): grad_normed_a = lax.psum(partial_norm, 'tensor')  57.8 us
    psum x1, waiting for transfers between devices, on_device(): lax.psum((scale_sum, shift_sum, proj_sum, proj_bias_sum, attn_sum_w, attn...  55.8 us
    all_gather x2, blocking collectives, backward_block(): grad_normed_b = lax.all_gather(grad_cols, 'tensor', axis=1, tiled=True)  37.9 us
    psum x1, blocking collectives, on_device(): lax.psum((scale_sum, shift_sum, proj_sum, proj_bias_sum, attn_sum_w, attn...  17.9 us
  transfers between devices with their start and end apart: 18, of which 16 were waited for; matrix products, arithmetic and copies ran while one was open for 10% of the time, Pallas kernels for 0%

profile of v1, /device:TPU:0, one launch (start us, length us, event | category | flops | bytes accessed | tf_op | source)
XLA Modules:
  0.0 808.0 jit_solution(6514185145795448324)
XLA Ops:
  18.0 52.4 %all-gather.7.cloned.1.call-done = f32[4,197,768]{2,1,0:T(8,128)} async-done(((f32[1,197,768]{2,1,0:T(8,128)}), f32[4,197,768]{2,1,0:T(8,128)}) %all-gather.7.cloned.1.call-update) | async-done | bytes 2420752 | tf_op jit(solution)/shard_map/all_gather | solution.py:15
  74.9 3.0 scatter_custom_fusion
  79.1 4.2 all-to-all-start
  83.4 12.5 %all-to-all-done = bf16[4,148,768]{2,1,0:T(8,128)(2,1)} async-done(((bf16[4,148,768]{2,1,0:T(8,128)(2,1)}), bf16[4,148,768]{2,1,0:T(8,128)(2,1)}, u32[]{:S(2)}, u32[]{:S(2)}) %all-to-all-start) | async-done | bytes 909344 | tf_op jit(solution)/shard_map/all_to_all | solution.py:157
  99.3 2.6 fusion.30
  101.9 4.3 copy.142
  106.2 4.5 reshape.725
  111.5 39.0 %reduce-scatter.13.cloned.1.call-done = f32[192,592]{1,0:T(8,128)} async-done(((f32[768,592]{1,0:T(8,128)}), f32[192,592]{1,0:T(8,128)}) %reduce-scatter.13.cloned.1.call-update) | async-done | bytes 454672
  154.7 29.3 %all_gather.26 = bf16[4,148,768]{1,0,2:T(4,128)(2,1)} all-gather(bf16[4,148,192]{1,0,2:T(4,128)(2,1)S(1)} %copy.93), channel_id=1, replica_groups=mesh['section'=2,'expert'=4,'tensor'=4] {'tensor'}, dimensions={2}, use_global_device_ids=true | all-gather | bytes 1136640 | tf_op jit(solution)/shard_map/all_gather | solution.py:169
  184.0 3.5 copy.94
  187.5 4.4 all-to-all-start.1
  192.8 10.1 %all-to-all-done.1 = bf16[4,148,768]{2,1,0:T(8,128)(2,1)} async-done(((bf16[4,148,768]{2,1,0:T(8,128)(2,1)}), bf16[4,148,768]{2,1,0:T(8,128)(2,1)}, u32[]{:S(2)}, u32[]{:S(2)}) %all-to-all-start.1) | async-done | bytes 909344 | tf_op jit(solution)/shard_map/all_to_all | solution.py:170
  204.3 2.7 gather_fusion
  207.0 2.8 reshape.627
  209.8 2.8 multiply_reduce_fusion.1
  219.9 52.4 %all-gather.9.cloned.1.call-done = f32[4,197,768]{2,1,0:T(8,128)} async-done(((f32[1,197,768]{2,1,0:T(8,128)}), f32[4,197,768]{2,1,0:T(8,128)}) %all-gather.9.cloned.1.call-update) | async-done | bytes 2420752 | tf_op jit(solution)/shard_map/all_gather | solution.py:15
  277.7 3.0 scatter_custom_fusion.1
  281.9 4.8 all-to-all-start.2
  288.3 3.0 mul.457
  291.4 3.3 scatter_custom_fusion.2
  295.8 3.4 all-to-all-done.2
  299.2 3.5 all-to-all-start.4
  302.8 4.6 multiply_convert_fusion
  307.4 7.3 all-to-all-done.4
  314.7 5.2 fusion.127
  323.0 4.3 copy.146
  327.3 4.5 reshape.729
  332.5 4.4 fusion.28
  336.9 4.3 copy.144
  341.2 4.5 reshape.727
  345.7 25.9 %reduce-scatter.17.cloned.1.call-done = f32[192,592]{1,0:T(8,128)} async-done(((f32[768,592]{1,0:T(8,128)}), f32[192,592]{1,0:T(8,128)}) %reduce-scatter.17.cloned.1.call-update) | async-done | bytes 454672
  374.0 4.1 all-to-all-start.5
  378.1 37.0 %reduce-scatter.15.cloned.1.call-done = f32[192,592]{1,0:T(8,128)} async-done(((f32[768,592]{1,0:T(8,128)}), f32[192,592]{1,0:T(8,128)}) %reduce-scatter.15.cloned.1.call-update) | async-done | bytes 454672
  419.3 29.3 %all_gather.29 = bf16[4,148,768]{1,0,2:T(4,128)(2,1)} all-gather(bf16[4,148,192]{1,0,2:T(4,128)(2,1)S(1)} %copy.96), channel_id=1, replica_groups=mesh['section'=2,'expert'=4,'tensor'=4] {'tensor'}, dimensions={2}, use_global_device_ids=true | all-gather | bytes 1136640 | tf_op jit(solution)/shard_map/all_gather | solution.py:169
  448.6 3.5 copy.97
  452.2 4.3 all-to-all-start.3
  462.6 19.6 %all_gather.30 = f32[197,768]{0,1:T(8,128)S(1)} all-gather(f32[197,192]{0,1:T(8,128)S(1)} %copy.100), channel_id=1, replica_groups=mesh['section'=2,'expert'=4,'tensor'=4] {'tensor'}, dimensions={1}, use_global_device_ids=true | all-gather | bytes 756480 | tf_op jit(solution)/shard_map/all_gather | solution.py:259
  484.6 2.7 gather_fusion.1
  487.2 2.8 reshape.628
  490.1 2.9 multiply_reduce_fusion
  500.9 39.6 %all-reduce.7.cloned.1.call-done = f32[197,768]{1,0:T(8,128)} async-done(((f32[197,768]{1,0:T(8,128)}), f32[197,768]{1,0:T(8,128)}) %all-reduce.7.cloned.1.call-update) | async-done | bytes 605200 | tf_op jit(solution)/shard_map/psum | solution.py:287
  544.9 2.6 collective-permute-done.1
  549.9 3.0 mul.490
  552.9 4.0 scatter_custom_fusion.3
  556.8 2.3 reshape.622
  559.1 17.6 %all_to_all.40 = bf16[4,148,768]{2,1,0:T(8,128)(2,1)S(1)} all-to-all(bf16[4,148,768]{2,1,0:T(8,128)(2,1)} %reshape.622), channel_id=1, replica_groups=mesh['section'=2,'expert'=4,'tensor'=4] {'expert'}, dimensions={0} | all-to-all | bytes 1818624 | tf_op jit(solution)/shard_map/all_to_all | solution.py:236
  576.8 4.9 fusion.128
  584.8 4.3 copy.148
  589.1 4.5 reshape.731
  595.0 4.1 fusion.61
  601.0 32.2 %reduce-scatter.19.cloned.1.call-done = f32[192,592]{1,0:T(8,128)} async-done(((f32[768,592]{1,0:T(8,128)}), f32[192,592]{1,0:T(8,128)}) %reduce-scatter.19.cloned.1.call-update) | async-done | bytes 454672
  635.6 3.7 all-to-all-start.7
  639.3 2.6 fusion.101
  641.8 2.9 all-to-all-done.7
  644.9 2.6 gather_fusion.3
  653.3 18.3 %all_gather.31 = f32[197,768]{0,1:T(8,128)} all-gather(f32[197,192]{0,1:T(8,128)} %copy.107), channel_id=1, replica_groups=mesh['section'=2,'expert'=4,'tensor'=4] {'tensor'}, dimensions={1}, use_global_device_ids=true | all-gather | bytes 756480 | tf_op jit(solution)/shard_map/all_gather | solution.py:259
  684.1 4.1 fusion.129
  688.6 2.6 copy.115
  692.7 4.3 fusion
  697.0 3.9 fusion.1
  701.3 18.2 %all-reduce.9.cloned.1.call-done = f32[197,768]{1,0:T(8,128)} async-done(((f32[197,768]{1,0:T(8,128)}), f32[197,768]{1,0:T(8,128)}) %all-reduce.9.cloned.1.call-update) | async-done | bytes 605200 | tf_op jit(solution)/shard_map/psum | solution.py:287
  723.7 17.9 %all-reduce.1 = (f32[1,2,768]{2,1,0:T(2,128)}, f32[1,2,768]{2,1,0:T(2,128)}, f32[1,2,192]{2,1,0:T(2,128)}, f32[1,768]{1,0:T(1,128)}) all-reduce(f32[1,2,768]{2,1,0:T(2,128)S(1)} %fusion.104, f32[1,2,768]{2,1,0:T(2,128)S(1)} %fusion.105, f32[1,2,192]{2,1,0:T(2,128)S(1)} %fusion.106, ...), channel_id=1, replica_groups=mesh['section'=2,'expert'=4,'tensor'=4] {'expert'}, use_global_device_ids=true, to_apply=%region_41.42 | all-reduce | flops 4224 | bytes 33792 | tf_op jit(solution)/shard_map/psum | solution.py:379
  741.6 55.8 %all-reduce.11.cloned.1.call-done = (f32[1,768,3,192]{1,3,2,0:T(8,128)}, f32[1,192,768]{2,1,0:T(8,128)}) async-done(((f32[1,768,3,192]{1,3,2,0:T(8,128)}, f32[1,192,768]{2,1,0:T(8,128)}), (f32[1,768,3,192]{1,3,2,0:T(8,128)}, f32[1,192,768]{2,1,0:T(8,128)})) %all-reduce.11.cloned.1.call-update) | async-done | bytes 2359312 | tf_op jit(solution)/shard_map/psum | solution.py:379
  797.3 2.9 copy.181
  (420 shorter events, 110.2 us)
Async XLA Ops:
  7.2 88.7 %copy-start = (bf16[1,1,768,768]{3,2,1,0:T(8,128)(2,1)S(1)}, bf16[1,1,768,768]{3,2,1,0:T(8,128)(2,1)}, u32[]{:S(2)}) copy-start(bf16[1,1,768,768]{3,2,1,0:T(8,128)(2,1)} %param.22) | copy-start | bytes 3538948
  7.2 63.2 %all-gather.7.cloned.1.call-start = ((), (), s32[]{:S(2)}) async-start(), calls=%async_computation.14 | async-start | bytes 3072000 | tf_op jit(solution)/shard_map/all_gather | solution.py:15
  8.5 4.9 copy-start.78
  8.5 4.9 copy-start.106
  13.6 203.8 %copy-start.65 = (f32[3,64]{1,0:T(4,128)}, f32[3,64]{1,0:T(4,128)S(1)}, u32[]{:S(2)}) copy-start(f32[3,64]{1,0:T(4,128)S(1)} %add.378) | copy-start | bytes 2308
  15.6 56.7 %copy-start.2 = (f32[1,197,768]{2,0,1:T(1,128)S(1)}, f32[1,197,768]{2,0,1:T(1,128)}, u32[]{:S(2)}) copy-start(f32[1,197,768]{2,0,1:T(1,128)} %param.14) | copy-start | bytes 1815556
  18.0 57.0 %copy-start.95 = (s32[394,1]{0,1:T(1,128)}, s32[394,1]{0,1:T(1,128)S(1)}, u32[]{:S(2)}) copy-start(s32[394,1]{0,1:T(1,128)S(1)} %compare_select_fusion) | copy-start | bytes 4732
  72.5 5.5 copy-start.71
  72.7 5.3 copy-start.87
  72.7 5.2 copy-start.79
  78.0 5.4 copy-start.105
  79.1 16.8 %all-to-all-start = ((bf16[4,148,768]{2,1,0:T(8,128)(2,1)}), bf16[4,148,768]{2,1,0:T(8,128)(2,1)}, u32[]{:S(2)}, u32[]{:S(2)}) async-start(bf16[4,148,768]{2,1,0:T(8,128)(2,1)} %reshape.612), calls=%async_computation | async-start | bytes 1867776 | tf_op jit(solution)/shard_map/all_to_all | solution.py:157
  83.3 67.2 %reduce-scatter.13.cloned.1.call-start = ((), (), s32[]{:S(2)}) async-start(), calls=%async_computation.16 | async-start | bytes 2457600
  83.4 14.7 %copy-start.101 = (f32[768]{0:T(1024)}, f32[768]{0:T(1024)S(1)}, u32[]{:S(2)}) copy-start(f32[768]{0:T(1024)S(1)} %reduce.20) | copy-start | bytes 9220
  111.5 43.2 %copy-start.89 = (f32[1,1,192]{2,1,0:T(1,128)}, f32[1,1,192]{2,1,0:T(1,128)S(1)}, u32[]{:S(2)}) copy-start(f32[1,1,192]{2,1,0:T(1,128)S(1)} %constant_dynamic-slice_fusion) | copy-start | bytes 2308
  184.0 8.0 copy-start.93
  184.0 8.8 %copy-start.96 = (s32[394,1]{0,1:T(1,128)S(1)}, s32[394,1]{0,1:T(1,128)}, u32[]{:S(2)}) copy-start(s32[394,1]{0,1:T(1,128)} %copy-done.95) | copy-start | bytes 4732
  187.5 15.4 %all-to-all-start.1 = ((bf16[4,148,768]{2,1,0:T(8,128)(2,1)}), bf16[4,148,768]{2,1,0:T(8,128)(2,1)}, u32[]{:S(2)}, u32[]{:S(2)}) async-start(bf16[4,148,768]{2,1,0:T(8,128)(2,1)} %copy.94), calls=%async_computation.1 | async-start | bytes 1867776 | tf_op jit(solution)/shard_map/all_to_all | solution.py:170
  192.0 80.3 %all-gather.9.cloned.1.call-start = ((), (), s32[]{:S(2)}) async-start(), calls=%async_computation.15 | async-start | bytes 3072000 | tf_op jit(solution)/shard_map/all_gather | solution.py:15
  212.7 3.1 collective-permute-start
  274.4 6.3 copy-start.73
  275.5 5.2 copy-start.83
  280.7 5.9 copy-start.94
  281.9 4.9 copy-start.27
  281.9 17.3 %all-to-all-start.2 = ((bf16[4,148,768]{2,1,0:T(8,128)(2,1)}), bf16[4,148,768]{2,1,0:T(8,128)(2,1)}, u32[]{:S(2)}, u32[]{:S(2)}) async-start(bf16[4,148,768]{2,1,0:T(8,128)(2,1)} %reshape.616), calls=%async_computation.2 | async-start | bytes 1867776 | tf_op jit(solution)/shard_map/all_to_all | solution.py:157
  291.4 4.4 copy-start.67
  299.2 15.4 %all-to-all-start.4 = ((bf16[4,148,768]{2,1,0:T(8,128)(2,1)}), bf16[4,148,768]{2,1,0:T(8,128)(2,1)S(1)}, u32[]{:S(2)}, u32[]{:S(2)}) async-start(bf16[4,148,768]{2,1,0:T(8,128)(2,1)} %reshape.618), calls=%async_computation.4 | async-start | bytes 1867776 | tf_op jit(solution)/shard_map/all_to_all | solution.py:236
  302.7 68.9 %reduce-scatter.17.cloned.1.call-start = ((), (), s32[]{:S(2)}) async-start(), calls=%async_computation.18 | async-start | bytes 2457600
  314.7 5.2 copy-start.19
  331.8 83.3 %reduce-scatter.15.cloned.1.call-start = ((), (), s32[]{:S(2)}) async-start(), calls=%async_computation.17 | async-start | bytes 2457600
  373.0 44.9 %copy-start.90 = (f32[1,1,192]{2,1,0:T(1,128)S(1)}, f32[1,1,192]{2,1,0:T(1,128)}, u32[]{:S(2)}) copy-start(f32[1,1,192]{2,1,0:T(1,128)} %copy-done.89) | copy-start | bytes 2308
  374.0 78.2 %all-to-all-start.5 = ((bf16[4,148,192]{2,1,0:T(8,128)(2,1)}), bf16[4,148,192]{2,1,0:T(8,128)(2,1)}, u32[]{:S(2)}, u32[]{:S(2)}) async-start(bf16[4,148,192]{2,1,0:T(8,128)(2,1)} %copy.147), calls=%async_computation.5 | async-start | bytes 622592 | tf_op jit(solution)/shard_map/all_to_all | solution.py:256
  448.6 8.0 copy-start.31
  448.6 8.0 copy-start.51
  448.6 8.0 copy-start.53
  448.6 8.0 copy-start.66
  452.2 5.2 copy-start.75
  452.2 31.0 %all-to-all-start.3 = ((bf16[4,148,768]{2,1,0:T(8,128)(2,1)}), bf16[4,148,768]{2,1,0:T(8,128)(2,1)}, u32[]{:S(2)}, u32[]{:S(2)}) async-start(bf16[4,148,768]{2,1,0:T(8,128)(2,1)} %copy.97), calls=%async_computation.3 | async-start | bytes 1867776 | tf_op jit(solution)/shard_map/all_to_all | solution.py:170
  456.5 84.0 %all-reduce.7.cloned.1.call-start = ((), (), s32[]{:S(2)}) async-start(), calls=%async_computation.12 | async-start | bytes 1228800 | tf_op jit(solution)/shard_map/psum | solution.py:287
  487.2 5.8 copy-start.4
  487.2 5.8 copy-start.72
  487.2 5.8 copy-start.74
  487.2 5.8 copy-start.80
  487.2 5.8 copy-start.84
  498.0 42.5 %copy-start.70 = (f32[197]{0:T(256)S(1)}, f32[197]{0:T(256)}, u32[]{:S(2)}) copy-start(f32[197]{0:T(256)} %copy-done.69) | copy-start | bytes 2368
  498.0 42.5 %copy-start.77 = (f32[197]{0:T(256)S(1)}, f32[197]{0:T(256)}, u32[]{:S(2)}) copy-start(f32[197]{0:T(256)} %copy-done.76) | copy-start | bytes 2368
  500.8 132.4 %reduce-scatter.19.cloned.1.call-start = ((), (), s32[]{:S(2)}) async-start(), calls=%async_computation.19 | async-start | bytes 2457600
  543.6 9.2 %copy-start.25 = (f32[197,768]{1,0:T(8,128)}, f32[197,768]{1,0:T(8,128)S(1)}, u32[]{:S(2)}) copy-start(f32[197,768]{1,0:T(8,128)S(1)} %multiply_add_fusion.4) | copy-start | bytes 1815556
  543.6 3.9 collective-permute-start.1
  548.4 4.4 copy-start.68
  556.8 19.9 %copy-start.103 = (f32[768]{0:T(1024)S(1)}, f32[768]{0:T(1024)}, u32[]{:S(2)}) copy-start(f32[768]{0:T(1024)} %copy-done.101) | copy-start | bytes 9220
  559.1 17.7 %copy-start.108 = (bf16[1,1,768,768]{3,2,1,0:T(8,128)(2,1)S(1)}, bf16[1,1,768,768]{3,2,1,0:T(8,128)(2,1)}, u32[]{:S(2)}) copy-start(bf16[1,1,768,768]{3,2,1,0:T(8,128)(2,1)} %param.24) | copy-start | bytes 3538948
  576.8 4.9 copy-start.20
  595.0 5.0 copy-start.6
  595.0 5.0 copy-start.42
  635.6 9.2 %all-to-all-start.7 = ((bf16[4,148,192]{2,1,0:T(8,128)(2,1)}), bf16[4,148,192]{2,1,0:T(8,128)(2,1)S(1)}, u32[]{:S(2)}, u32[]{:S(2)}) async-start(bf16[4,148,192]{2,1,0:T(8,128)(2,1)} %copy.149), calls=%async_computation.7 | async-start | bytes 622592 | tf_op jit(solution)/shard_map/all_to_all | solution.py:256
  639.3 80.2 %all-reduce.9.cloned.1.call-start = ((), (), s32[]{:S(2)}) async-start(), calls=%async_computation.13 | async-start | bytes 1228800 | tf_op jit(solution)/shard_map/psum | solution.py:287
  647.4 26.4 %copy-start.8 = (f32[197,768]{1,0:T(8,128)S(1)}, f32[197,768]{1,0:T(8,128)}, u32[]{:S(2)}) copy-start(f32[197,768]{1,0:T(8,128)} %copy-done.7) | copy-start | bytes 1815556
  680.8 116.5 %all-reduce.11.cloned.1.call-start = ((), (), s32[]{:S(2)}) async-start(), calls=%async_computation.20 | async-start | bytes 4718592 | tf_op jit(solution)/shard_map/psum | solution.py:379
  684.1 4.4 copy-start.91
  684.1 4.5 copy-start.92
  692.7 4.4 copy-start.112
  692.7 4.4 copy-start.113
  700.9 19.9 %copy-start.81 = (f32[197]{0:T(256)S(1)}, f32[197]{0:T(256)}, u32[]{:S(2)}) copy-start(f32[197]{0:T(256)} %get-tuple-element.115) | copy-start | bytes 2368
  (69 other events, 149.6 us)
Sparse Core Ops, SparseCore 0:
  15.7 54.6 all-gather.6
  110.9 39.6 reduce-scatter.12
  220.0 52.2 all-gather.8
  332.0 39.6 reduce-scatter.16
  374.4 40.6 reduce-scatter.14
  501.0 39.4 all-reduce.6
  593.7 39.4 reduce-scatter.18
  680.9 38.4 all-reduce.8
  723.2 74.1 all-reduce.10
